TPU v7x, 256 devices: a whole 4x4x8 slice. The times are simulated.
256 devices in a mesh: sweep: 4 (over y), xsec: 64 (over x, z, core).
Axes of the slice: x: 4, y: 4, z: 8, core: 2. Of those that a mesh axis runs over, the one named last changes fastest.
Arguments:
- cond_block: bfloat16 [4, 64, 2, 24, 40, 512], P('sweep', 'xsec'), may hold values from -0.15625 to 0.15625
- interior_src: bfloat16 [4, 64, 2, 4, 40, 512], P('sweep', 'xsec'), may hold values from -6 to 6
- face_index: int32 [4, 64, 64, 192], P('sweep', 'xsec'), may hold values from 0 to 255
- owner_count: int32 [4, 64, 64], P('sweep', 'xsec'), may hold values from 1 to 8, as said below
- coupling: float32 [8, 2, 8192], P('sweep', None, 'xsec'), may hold values from -1 to 1
- schur_inv: bfloat16 [8, 2, 8192, 8192], P('sweep', None, None, 'xsec'), may hold values from -0.046875 to 0.046875
Outputs:
- sweep_sol: float32 [8, 8, 8192], P('sweep', None, 'xsec')
Inputs may be any that keep to these rules, and one draw needn't show every extreme that they name: `owner_count`: every count is at least 1 and at most 8; in each sweep row some owner receives 8 live slots from every sender.
All inputs are finite; a program needn't handle non-finite values.
Results may differ from a plain program's by a relative error of at most 0.006.
Values may be sent and summed in bfloat16 or wider, within the bound.
A program may use at most 64 MiB of HBM per device.

v0:
```python
from functools import partial

import jax
import jax.numpy as jnp
from jax import lax
from jax.sharding import PartitionSpec as P

CAP = 8


def from_behind(value, axis, steps):
    count = lax.axis_size(axis)
    initial, last = (max(0, -steps), min(count, count - steps))
    return lax.ppermute(value, axis, [(source, source + steps) for source in range(initial, last)])


def in_order(pieces, dim):
    pieces = jnp.moveaxis(pieces, 0, dim)
    shape = pieces.shape
    return pieces.reshape(*shape[:dim], shape[dim] * shape[dim + 1], *shape[dim + 2 :])


def copy_for_each(value, axis):
    copies = jnp.broadcast_to(value, (lax.axis_size(axis), *value.shape))
    return lax.all_to_all(copies, axis, split_axis=0, concat_axis=0, tiled=True)


def gathered_copies(value, axis, dim):
    return in_order(copy_for_each(value, axis), dim)


def combine_rows(totals, pieces, first_row, schur_layer):
    return (
        jnp.dot(pieces, schur_layer[0], preferred_element_type=jnp.float32),
        jnp.dot(pieces, schur_layer[1], preferred_element_type=jnp.float32),
    )


def layer_input(loads, incoming, coupling_layer):
    real_part = loads[0] - (coupling_layer[0] * incoming[0] - coupling_layer[1] * incoming[1])
    imag_part = loads[1] - (coupling_layer[0] * incoming[1] + coupling_layer[1] * incoming[0])
    return jnp.concatenate([real_part, imag_part], 0).astype(jnp.bfloat16)


def layer_output(totals, count):
    first, second = totals
    return jnp.stack([first[:count] - second[count:], second[:count] + first[count:]], 0)


def shards(cond_block, interior_src, face_index, owner_count, coupling, schur_inv):
    layers_here = schur_inv.shape[0]
    width = schur_inv.shape[3]
    sources = interior_src.shape[3]
    n_faces = cond_block.shape[3]
    n_inner = cond_block.shape[4]
    peers = lax.axis_size("xsec")
    face_rows_len = n_faces * CAP
    couple_blocks = cond_block[0, 0].reshape(2, n_faces, n_inner, peers, CAP)
    interior = interior_src[0, 0].reshape(2, sources, n_inner, peers, CAP)

    def contract(first, second):
        return jnp.einsum("kidp,sidp->dskp", first, second, preferred_element_type=jnp.float32)

    real_part = contract(couple_blocks[0], interior[0]) - contract(couple_blocks[1], interior[1])
    imag_part = contract(couple_blocks[0], interior[1]) + contract(couple_blocks[1], interior[0])
    outgoing_rows = jnp.stack([real_part, imag_part], 1).reshape(peers, 2 * sources, face_rows_len)
    index_rows = face_index[0, 0]
    positions = jnp.arange(face_rows_len) % CAP
    live_mask = positions[None, :] < owner_count[0, 0][:, None]
    slot_ids = jnp.arange(layers_here * width)
    received = lax.all_to_all(outgoing_rows, "xsec", split_axis=0, concat_axis=0, tiled=True)
    row_count = received.shape[1]

    def add_group(group_at, running):
        values_block = lax.dynamic_slice_in_dim(received, group_at * 8, 8, 0)
        index_block = lax.dynamic_slice_in_dim(index_rows, group_at * 8, 8, 0)
        mask_block = lax.dynamic_slice_in_dim(live_mask, group_at * 8, 8, 0)
        onehot = jnp.where(
            (index_block[:, :, None] == slot_ids[None, None, :]) & mask_block[:, :, None], 1.0, 0.0
        ).astype(jnp.float32)
        return running + jnp.einsum(
            "cmf,cfz->mz", values_block, onehot, precision=lax.Precision.HIGHEST
        )

    start_sum = jnp.zeros((row_count, layers_here * width), jnp.float32)
    assembled = lax.fori_loop(0, peers // 8, add_group, start_sum)
    loads_all = assembled.reshape(2, sources, layers_here, width)
    chain = lax.axis_size("sweep")
    outgoing = jnp.zeros((2, sources, width), jnp.float32)
    layers_out = []
    for round_at in range(chain):
        incoming = from_behind(outgoing, "sweep", 1)
        carried = incoming
        layers_out = []
        for layer_at in range(layers_here):
            folder = partial(combine_rows, schur_layer=schur_inv[layer_at])
            empty = jnp.zeros((2 * sources, width), jnp.float32)
            totals = folder(
                (empty, empty),
                gathered_copies(
                    layer_input(loads_all[:, :, layer_at], carried, coupling[layer_at]), "xsec", 1
                ),
                jnp.int32(0),
            )
            carried = layer_output(totals, sources)
            layers_out.append(carried)
        outgoing = carried
    solved = jnp.stack(layers_out, 0)
    return solved.reshape(layers_here, 2 * sources, width)


def solution(mesh):
    placed = (
        P("sweep", "xsec", None, None, None, None),
        P("sweep", "xsec", None, None, None, None),
        P("sweep", "xsec", None, None),
        P("sweep", "xsec", None),
        P("sweep", None, "xsec"),
        P("sweep", None, None, "xsec"),
    )
    return jax.shard_map(
        shards, mesh=mesh, in_specs=placed, out_specs=P("sweep", None, "xsec"), check_vma=False
    )
```

profile of v0, /device:TPU:25, one launch (start us, length us, event | category | flops | bytes accessed | tf_op | source)
XLA Modules:
  0.0 242.4 jit_solution(9395540681642031992)
XLA Ops:
  0.0 2.9 %fusion.88 = (bf16[1,1,1,24,40,512]{5,4,3,2,1,0:T(8,128)(2,1)}, bf16[1,1,1,24,40,512]{5,4,3,2,1,0:T(8,128)(2,1)}) fusion(bf16[1,1,2,24,40,512]{5,4,3,2,1,0:T(8,128)(2,1)} %param.8), kind=kLoop, calls=%fused_computation.148 | loop fusion | bytes 3932160 | tf_op jit(solution)/shard_map/slice | solution.py:64
  2.9 3.7 %copy.22 = bf16[1,1,1,24,40,512]{4,3,5,2,1,0:T(8,128)(2,1)S(1)} copy(bf16[1,1,1,24,40,512]{5,4,3,2,1,0:T(8,128)(2,1)} %get-tuple-element.151) | data formatting | bytes 1966080 | tf_op jit(solution)/shard_map/slice | solution.py:64
  8.8 4.6 %copy.24 = bf16[1,1,1,24,40,512]{4,3,5,2,1,0:T(8,128)(2,1)} copy(bf16[1,1,1,24,40,512]{5,4,3,2,1,0:T(8,128)(2,1)} %get-tuple-element.150) | data formatting | bytes 1966080 | tf_op jit(solution)/shard_map/slice | solution.py:64
  14.5 2.8 %fusion.91 = f32[64,8,4,24]{3,2,1,0:T(4,128)S(1)} fusion(bf16[4,40,64,8]{1,0,3,2:T(4,128)(2,1)} %bitcast.217, bf16[24,40,64,8]{1,0,3,2:T(8,128)(2,1)S(1)} %bitcast.213), kind=kOutput, calls=%fused_computation.151 | convolution fusion | flops 3932160 | bytes 1343488 | tf_op jit(solution)/shard_map/kidp,sidp->dskp/dot_general | solution.py:62
  17.3 2.7 %fusion.92 = f32[64,8,4,24]{3,2,1,0:T(4,128)} fusion(bf16[4,40,64,8]{1,0,3,2:T(4,128)(2,1)S(1)} %bitcast.219, bf16[24,40,64,8]{1,0,3,2:T(8,128)(2,1)S(1)} %bitcast.214), kind=kOutput, calls=%fused_computation.152 | convolution fusion | flops 3932160 | bytes 1343488 | tf_op jit(solution)/shard_map/kidp,sidp->dskp/dot_general | solution.py:62
  20.0 2.8 %fusion.53 = f32[64,1,4,24,8]{3,2,4,0,1:T(4,128)} fusion(f32[64,8,4,24]{3,2,1,0:T(4,128)S(1)} %fusion.91, bf16[4,40,64,8]{1,0,3,2:T(4,128)(2,1)S(1)} %bitcast.220, bf16[24,40,64,8]{1,0,3,2:T(8,128)(2,1)S(1)} %bitcast.215), kind=kOutput, calls=%fused_computation.52 | convolution fusion | flops 3981312 | bytes 1540096 | tf_op jit(solution)/shard_map/kidp,sidp->dskp/dot_general | solution.py:62
  24.6 4.1 %fusion.52 = f32[64,1,4,24,8]{3,2,4,0,1:T(4,128)} fusion(f32[64,8,4,24]{3,2,1,0:T(4,128)} %fusion.92, bf16[4,40,64,8]{1,0,3,2:T(4,128)(2,1)} %bitcast.218, bf16[24,40,64,8]{1,0,3,2:T(8,128)(2,1)S(1)} %bitcast.216), kind=kOutput, calls=%fused_computation.50 | convolution fusion | flops 3981312 | bytes 1540096 | tf_op jit(solution)/shard_map/kidp,sidp->dskp/dot_general | solution.py:62
  31.8 12.2 %all-to-all-start = ((f32[64,8,192]{2,1,0:T(8,128)}), f32[64,8,192]{2,1,0:T(8,128)S(1)}, u32[]{:S(2)}, u32[]{:S(2)}) async-start(f32[64,8,192]{2,1,0:T(8,128)} %copy.27), calls=%async_computation | async-start | bytes 1048576 | tf_op jit(solution)/shard_map/all_to_all | solution.py:71
  45.4 15.8 %all-to-all-done = f32[64,8,192]{2,1,0:T(8,128)S(1)} async-done(((f32[64,8,192]{2,1,0:T(8,128)}), f32[64,8,192]{2,1,0:T(8,128)S(1)}, u32[]{:S(2)}, u32[]{:S(2)}) %all-to-all-start) | async-done | bytes 393248 | tf_op jit(solution)/shard_map/all_to_all | solution.py:71
  61.2 20.3 %while.14 = (s32[]{:T(128)}, f32[8,256]{1,0:T(8,128)S(1)}, f32[64,8,192]{2,1,0:T(8,128)S(1)}, s32[64,192]{1,0:T(8,128)}, pred[64,192]{1,0:T(8,128)(4,1)S(1)}, /*index=5*/s32[]{:T(128)}, s32[]{:T(128)}, s32[]{:T(128)}, s32[]{:T(128)}) while((s32[]{:T(128)}, f32[8,256]{1,0:T(8,128)S(1)}, f32[64,8,192]{2,1,0:T(8,128)S(1)}, ...), condition=%wide.region_1.2_spmd.clone, body=%wide.region_0.1_spmd.clone.sunk | while | flops 38932488 | bytes 107681 | solution.py:86
  81.7 16.4 %all_to_all.45 = bf16[64,8,128]{2,1,0:T(8,128)(2,1)S(1)} all-to-all(bf16[64,8,128]{2,1,0:T(8,128)(2,1)S(1)} %broadcast_in_dim.58), channel_id=1, replica_groups=mesh['sweep'=4,'xsec'=64] {'xsec'}, dimensions={0} | all-to-all | bytes 262144 | tf_op jit(solution)/shard_map/all_to_all | solution.py:25
  98.1 2.1 fusion.42
  102.3 15.0 %all_to_all.46 = bf16[64,8,128]{2,1,0:T(8,128)(2,1)S(1)} all-to-all(bf16[64,8,128]{2,1,0:T(8,128)(2,1)S(1)} %broadcast_in_dim.59), channel_id=1, replica_groups=mesh['sweep'=4,'xsec'=64] {'xsec'}, dimensions={0} | all-to-all | bytes 262144 | tf_op jit(solution)/shard_map/all_to_all | solution.py:25
  119.2 2.1 fusion.34
  122.7 3.1 %collective-permute-done.1 = f32[2,4,128]{2,1,0:T(4,128)S(1)} collective-permute-done((f32[2,4,128]{2,1,0:T(4,128)S(1)}, f32[2,4,128]{2,1,0:T(4,128)S(1)}, u32[]{:S(2)}, u32[]{:S(2)}) %collective-permute-start.1) | collective-permute-done | bytes 4128 | tf_op jit(solution)/shard_map/ppermute | solution.py:14
  125.8 16.2 %all_to_all.47 = bf16[64,8,128]{2,1,0:T(8,128)(2,1)S(1)} all-to-all(bf16[64,8,128]{2,1,0:T(8,128)(2,1)S(1)} %broadcast_in_dim.60), channel_id=1, replica_groups=mesh['sweep'=4,'xsec'=64] {'xsec'}, dimensions={0} | all-to-all | bytes 262144 | tf_op jit(solution)/shard_map/all_to_all | solution.py:25
  146.0 15.0 %all_to_all.48 = bf16[64,8,128]{2,1,0:T(8,128)(2,1)S(1)} all-to-all(bf16[64,8,128]{2,1,0:T(8,128)(2,1)S(1)} %broadcast_in_dim.61), channel_id=1, replica_groups=mesh['sweep'=4,'xsec'=64] {'xsec'}, dimensions={0} | all-to-all | bytes 262144 | tf_op jit(solution)/shard_map/all_to_all | solution.py:25
  164.7 3.1 %collective-permute-done.2 = f32[2,4,128]{2,1,0:T(4,128)S(1)} collective-permute-done((f32[2,4,128]{2,1,0:T(4,128)S(1)}, f32[2,4,128]{2,1,0:T(4,128)S(1)}, u32[]{:S(2)}, u32[]{:S(2)}) %collective-permute-start.2) | collective-permute-done | bytes 4128 | tf_op jit(solution)/shard_map/ppermute | solution.py:14
  167.8 16.2 %all_to_all.49 = bf16[64,8,128]{2,1,0:T(8,128)(2,1)S(1)} all-to-all(bf16[64,8,128]{2,1,0:T(8,128)(2,1)S(1)} %broadcast_in_dim.62), channel_id=1, replica_groups=mesh['sweep'=4,'xsec'=64] {'xsec'}, dimensions={0} | all-to-all | bytes 262144 | tf_op jit(solution)/shard_map/all_to_all | solution.py:25
  184.8 15.0 %all_to_all.50 = bf16[64,8,128]{2,1,0:T(8,128)(2,1)S(1)} all-to-all(bf16[64,8,128]{2,1,0:T(8,128)(2,1)S(1)} %broadcast_in_dim.63), channel_id=1, replica_groups=mesh['sweep'=4,'xsec'=64] {'xsec'}, dimensions={0} | all-to-all | bytes 262144 | tf_op jit(solution)/shard_map/all_to_all | solution.py:25
  201.9 3.1 %collective-permute-done.3 = f32[2,4,128]{2,1,0:T(4,128)S(1)} collective-permute-done((f32[2,4,128]{2,1,0:T(4,128)S(1)}, f32[2,4,128]{2,1,0:T(4,128)S(1)}, u32[]{:S(2)}, u32[]{:S(2)}) %collective-permute-start.3) | collective-permute-done | bytes 4128 | tf_op jit(solution)/shard_map/ppermute | solution.py:14
  205.0 16.2 %all_to_all.51 = bf16[64,8,128]{2,1,0:T(8,128)(2,1)S(1)} all-to-all(bf16[64,8,128]{2,1,0:T(8,128)(2,1)S(1)} %broadcast_in_dim.64), channel_id=1, replica_groups=mesh['sweep'=4,'xsec'=64] {'xsec'}, dimensions={0} | all-to-all | bytes 262144 | tf_op jit(solution)/shard_map/all_to_all | solution.py:25
  222.6 4.9 %all-to-all-start.8 = ((bf16[64,8,128]{2,1,0:T(8,128)(2,1)}), bf16[64,8,128]{2,1,0:T(8,128)(2,1)S(1)}, u32[]{:S(2)}, u32[]{:S(2)}) async-start(bf16[64,8,128]{2,1,0:T(8,128)(2,1)} %broadcast_in_dim.65), calls=%async_computation.8 | async-start | bytes 262144 | tf_op jit(solution)/shard_map/all_to_all | solution.py:25
  227.5 10.3 %all-to-all-done.8 = bf16[64,8,128]{2,1,0:T(8,128)(2,1)S(1)} async-done(((bf16[64,8,128]{2,1,0:T(8,128)(2,1)}), bf16[64,8,128]{2,1,0:T(8,128)(2,1)S(1)}, u32[]{:S(2)}, u32[]{:S(2)}) %all-to-all-start.8) | async-done | bytes 131104 | tf_op jit(solution)/shard_map/all_to_all | solution.py:25
  (106 shorter events, 51.7 us)
Async XLA Ops:
  14.5 2.8 %copy-start.2 = (bf16[1,1,1,4,40,512]{4,3,5,2,1,0:T(4,128)(2,1)S(1)}, bf16[1,1,1,4,40,512]{4,3,5,2,1,0:T(4,128)(2,1)}, u32[]{:S(2)}) copy-start(bf16[1,1,1,4,40,512]{4,3,5,2,1,0:T(4,128)(2,1)} %copy.23) | copy-start | bytes 491524
  17.3 2.7 %copy-start = (bf16[1,1,1,24,40,512]{4,3,5,2,1,0:T(8,128)(2,1)S(1)}, bf16[1,1,1,24,40,512]{4,3,5,2,1,0:T(8,128)(2,1)}, u32[]{:S(2)}) copy-start(bf16[1,1,1,24,40,512]{4,3,5,2,1,0:T(8,128)(2,1)} %copy.24) | copy-start | bytes 2949124
  20.0 4.6 %copy-start.1 = (bf16[1,1,1,24,40,512]{4,3,5,2,1,0:T(8,128)(2,1)S(1)}, bf16[1,1,1,24,40,512]{4,3,5,2,1,0:T(8,128)(2,1)}, u32[]{:S(2)}) copy-start(bf16[1,1,1,24,40,512]{4,3,5,2,1,0:T(8,128)(2,1)} %copy.24) | copy-start | bytes 2949124
  28.7 16.6 %copy-start.3 = (f32[2,2,128]{2,1,0:T(2,128)S(1)}, f32[2,2,128]{2,1,0:T(2,128)}, u32[]{:S(2)}) copy-start(f32[2,2,128]{2,1,0:T(2,128)} %param.12) | copy-start | bytes 6148
  28.7 16.6 %copy-start.4 = (s32[1,1,64]{2,1,0:T(1,128)S(1)}, s32[1,1,64]{2,1,0:T(1,128)}, u32[]{:S(2)}) copy-start(s32[1,1,64]{2,1,0:T(1,128)} %param.11) | copy-start | bytes 772
  31.8 29.4 %all-to-all-start = ((f32[64,8,192]{2,1,0:T(8,128)}), f32[64,8,192]{2,1,0:T(8,128)S(1)}, u32[]{:S(2)}, u32[]{:S(2)}) async-start(f32[64,8,192]{2,1,0:T(8,128)} %copy.27), calls=%async_computation | async-start | bytes 1048576 | tf_op jit(solution)/shard_map/all_to_all | solution.py:71
  43.9 37.7 %collective-permute-start = (f32[2,4,128]{2,1,0:T(4,128)S(1)}, f32[2,4,128]{2,1,0:T(4,128)S(1)}, u32[]{:S(2)}, u32[]{:S(2)}) collective-permute-start(f32[2,4,128]{2,1,0:T(4,128)S(1)} %broadcast_in_dim.57), channel_id=1, source_target_pairs={{0,64},{64,128},{128,192},{1,65},{65,129},{129,193},{2,66},{66,130... | collective-permute-start | bytes 12296 | tf_op jit(solution)/shard_map/ppermute | solution.py:14
  98.1 64.9 %slice-start = ((s8[8388608]{0:T(1024)(128)(4,1)}), s8[4194304]{0:T(1024)(128)(4,1)S(1)}, s32[]{:S(2)}) async-start(s8[8388608]{0:T(1024)(128)(4,1)} %bitcast.211), calls=%async_computation.9 | async-start | bytes 8388608
  119.2 43.7 %slice-start.1 = ((s8[8388608]{0:T(1024)(128)(4,1)}), s8[4194304]{0:T(1024)(128)(4,1)S(1)}, s32[]{:S(2)}) async-start(s8[8388608]{0:T(1024)(128)(4,1)} %bitcast.211), calls=%async_computation.10 | async-start | bytes 8388608
  121.4 4.4 %collective-permute-start.1 = (f32[2,4,128]{2,1,0:T(4,128)S(1)}, f32[2,4,128]{2,1,0:T(4,128)S(1)}, u32[]{:S(2)}, u32[]{:S(2)}) collective-permute-start(f32[2,4,128]{2,1,0:T(4,128)S(1)} %pad_maximum_fusion.2), channel_id=1, source_target_pairs={{0,64},{64,128},{128,192},{1,65},{65,129},{129,193},{2,66},{66,130... | collective-permute-start | bytes 12296 | tf_op jit(solution)/shard_map/ppermute | solution.py:14
  163.4 4.4 %collective-permute-start.2 = (f32[2,4,128]{2,1,0:T(4,128)S(1)}, f32[2,4,128]{2,1,0:T(4,128)S(1)}, u32[]{:S(2)}, u32[]{:S(2)}) collective-permute-start(f32[2,4,128]{2,1,0:T(4,128)S(1)} %pad_maximum_fusion.3), channel_id=1, source_target_pairs={{0,64},{64,128},{128,192},{1,65},{65,129},{129,193},{2,66},{66,130... | collective-permute-start | bytes 12296 | tf_op jit(solution)/shard_map/ppermute | solution.py:14
  200.6 4.4 %collective-permute-start.3 = (f32[2,4,128]{2,1,0:T(4,128)S(1)}, f32[2,4,128]{2,1,0:T(4,128)S(1)}, u32[]{:S(2)}, u32[]{:S(2)}) collective-permute-start(f32[2,4,128]{2,1,0:T(4,128)S(1)} %pad_maximum_fusion.4), channel_id=1, source_target_pairs={{0,64},{64,128},{128,192},{1,65},{65,129},{129,193},{2,66},{66,130... | collective-permute-start | bytes 12296 | tf_op jit(solution)/shard_map/ppermute | solution.py:14
  222.6 15.2 %all-to-all-start.8 = ((bf16[64,8,128]{2,1,0:T(8,128)(2,1)}), bf16[64,8,128]{2,1,0:T(8,128)(2,1)S(1)}, u32[]{:S(2)}, u32[]{:S(2)}) async-start(bf16[64,8,128]{2,1,0:T(8,128)(2,1)} %broadcast_in_dim.65), calls=%async_computation.8 | async-start | bytes 262144 | tf_op jit(solution)/shard_map/all_to_all | solution.py:25
where the time goes:
time: 244 us; the launch traced here: 242 us
  blocking collectives  110 us (45%)
  matrix products  47.7 us (20%)
  waiting for transfers between devices  35.3 us (14%)
  local copies, waits for them, and re-layouts  25.7 us (11%)
  starting transfers between devices  22.2 us (9%)
    all_to_all x7, blocking collectives, copy_for_each(): return lax.all_to_all(copies, axis, split_axis=0, concat_axis=0, tiled=True)  110 us
    all_to_all x1, waiting for transfers between devices, shards(): lax.all_to_all(outgoing_rows, 'xsec', split_axis=0, concat_axis=0, tiled=...  15.8 us
    dot_general x8, matrix products, add_group(): jnp.einsum('cmf,cfz->mz', values_block, onehot, precision=lax.Precision.H...  14.6 us
    dot_general x4, matrix products, contract(): jnp.einsum('kidp,sidp->dskp', first, second, preferred_element_type=jnp.f...  12.4 us
    all_to_all x1, starting transfers between devices, shards(): lax.all_to_all(outgoing_rows, 'xsec', split_axis=0, concat_axis=0, tiled=...  12.2 us
    dot_general x8, matrix products, combine_rows(): jnp.dot(pieces, schur_layer[1], preferred_element_type=jnp.float32)  11.1 us
    all_to_all x1, waiting for transfers between devices, copy_for_each(): return lax.all_to_all(copies, axis, split_axis=0, concat_axis=0, tiled=True)  10.3 us
    dot_general x8, matrix products, combine_rows(): jnp.dot(pieces, schur_layer[0], preferred_element_type=jnp.float32)  9.59 us
  transfers between devices with their start and end apart: 6, of which 5 were waited for; matrix products, arithmetic and copies ran while one was open for 8% of the time, Pallas kernels for 0%

commit v1 on v0

v1 whole, which is shorter than its diff:
```python
import functools

import jax
import jax.numpy as jnp
from jax import lax
from jax.experimental import pallas as pl
from jax.experimental.pallas import tpu as pltpu
from jax.sharding import PartitionSpec as P

CAP = 8
MESH = pl.DeviceIdType.MESH
NX, NZ = 4, 8
DX_ORDER = (2, 1, 3, 0)
DZ_ORDER = (4, 3, 5, 2, 6, 1, 7, 0)


def peers_far_first():
    offsets = [(dx, dz, dc) for dx in range(NX) for dz in range(NZ) for dc in range(2)]
    offsets.remove((0, 0, 0))
    return sorted(offsets, key=lambda o: -(min(o[0], NX - o[0]) + min(o[1], NZ - o[1])))


def row_iota(shape):
    return lax.broadcasted_iota(jnp.int32, shape, 0)


def lane_iota(shape):
    return lax.broadcasted_iota(jnp.int32, shape, 1)


def sum_rows(parts):
    rows = row_iota((8, 128))
    top = rows < 4
    level = [
        jnp.where(top, parts[m], parts[m + 4])
        + pltpu.roll(jnp.where(top, parts[m + 4], parts[m]), 4, 0)
        for m in range(4)
    ]
    for step in (2, 1):
        low = (rows & step) == 0
        level = [
            jnp.where(
                low,
                level[m] + pltpu.roll(level[m], 8 - step, 0),
                level[m + step] + pltpu.roll(level[m + step], step, 0),
            )
            for m in range(step)
        ]
    return level[0]


def swap_groups(values, steps):
    groups = lane_iota((8, 128)) // CAP
    values = list(values)
    for step in steps:
        upper = (groups & step) != 0
        for at in range(len(values)):
            if at & step:
                continue
            first, second = values[at], values[at + step]
            values[at] = jnp.where(upper, pltpu.roll(second, step * CAP, 1), first)
            values[at + step] = jnp.where(upper, second, pltpu.roll(first, 128 - step * CAP, 1))
    return values


def kernel(
    count, inter, face, coup, cond, schur, out,
    cond_v, schur_v, inter_f, terms, send_v, recv_v, onehot,
    rhs_v, gath_v, u_send, u_recv,
    cond_sem, schur_sem, a2a_send, a2a_recv, rhs_send, rhs_recv, usend_sem, urecv_sem,
):
    me = lax.axis_index("xsec")
    row = lax.axis_index("sweep")
    mx, mz, mc = me // 16, (me // 2) % 8, me % 2
    n_faces = cond.shape[1]
    layers = schur.shape[0]

    def tile_of(dx):
        return (mx + dx) % NX

    def peer(offset):
        dx, dz, dc = offset
        return tile_of(dx) * 16 + ((mz + dz) % NZ) * 2 + (mc + dc) % 2

    def lanes_of(dx):
        return pl.ds(pl.multiple_of(tile_of(dx) * 128, 128), 128)

    cond_copies = [
        pltpu.make_async_copy(
            cond.at[:, :, :, lanes_of(dx)], cond_v.at[:, :, :, lanes_of(dx)], cond_sem.at[at]
        )
        for at, dx in enumerate(DX_ORDER)
    ]
    for copy in cond_copies:
        copy.start()
    schur_copies = [
        pltpu.make_async_copy(schur.at[layer], schur_v.at[layer], schur_sem.at[layer])
        for layer in range(layers)
    ]
    for copy in schur_copies:
        copy.start()

    order = peers_far_first()
    barrier = pltpu.get_barrier_semaphore()
    for offset in order:
        pl.semaphore_signal(barrier, inc=1, device_id=(row, peer(offset)), device_id_type=MESH)
    pl.semaphore_signal(barrier, inc=1, device_id=((row + 1) % 4, me), device_id_type=MESH)
    pl.semaphore_signal(barrier, inc=1, device_id=((row + 3) % 4, me), device_id_type=MESH)

    for at, dx in enumerate(DX_ORDER):
        lanes = lanes_of(dx)
        inter_f[...] = inter[:, :, :, lanes].astype(jnp.float32)
        cond_copies[at].wait()

        def one_face(k, carry):
            real = cond_v[0, k, :, lanes].astype(jnp.float32)
            imag = cond_v[1, k, :, lanes].astype(jnp.float32)

            def fold(value):
                return sum(value[8 * v : 8 * v + 8] for v in range(value.shape[0] // 8))

            real_parts = [fold(real * inter_f[0, j] - imag * inter_f[1, j]) for j in range(4)]
            imag_parts = [fold(real * inter_f[1, j] + imag * inter_f[0, j]) for j in range(4)]
            terms[k] = sum_rows(real_parts + imag_parts)
            return carry

        lax.fori_loop(0, n_faces, one_face, 0, unroll=4)
        first = swap_groups([terms[k] for k in range(16)], (8, 4, 2, 1))
        second = swap_groups([terms[k] for k in range(16, 24)], (4, 2, 1))
        base = tile_of(dx) * 16
        for d in range(16):
            tail = second[d % 8] if d < 8 else pltpu.roll(second[d % 8], 64, 1)
            send_v[base + d] = jnp.concatenate([first[d], tail], 1).astype(jnp.bfloat16)
        if at == 0:
            pl.semaphore_wait(barrier, len(order) + 2)
        for dz in DZ_ORDER:
            for dc in range(2):
                if (dx, dz, dc) == (0, 0, 0):
                    continue
                target = peer((dx, dz, dc))
                pltpu.make_async_remote_copy(
                    src_ref=send_v.at[target], dst_ref=recv_v.at[me],
                    send_sem=a2a_send, recv_sem=a2a_recv,
                    device_id=(row, target), device_id_type=MESH,
                ).start()
    recv_v[me] = send_v[me]

    slots = onehot.shape[1]
    columns = lane_iota((1, 256))
    place = columns % CAP
    unknown = row_iota((slots, 256))

    def one_sender(c, carry):
        index = jnp.concatenate([face[pl.ds(c, 1), :], jnp.full((1, 64), -1, jnp.int32)], 1)
        index = jnp.where(place < count[0, c], index, -1)
        onehot[c] = jnp.where(unknown == index, 1.0, 0.0).astype(jnp.bfloat16)
        return carry

    senders = recv_v.shape[0]
    lax.fori_loop(0, senders, one_sender, 0)

    others = pl.ds(0, senders - 1)
    pltpu.make_async_copy(recv_v.at[others], recv_v.at[others], a2a_recv).wait()

    def add_sender(c, total):
        return total + lax.dot_general(
            recv_v[c], onehot[c], (((1,), (1,)), ((), ())), preferred_element_type=jnp.float32
        )

    loads = lax.fori_loop(0, senders, add_sender, jnp.zeros((8, slots), jnp.float32), unroll=8)

    sign = jnp.where(row_iota((8, 128)) < 4, -1.0, 1.0)

    def turned(value):
        return sign * pltpu.roll(value, 4, 0)

    @pl.when(row == 0)
    def _():
        u_recv[...] = jnp.zeros_like(u_recv)

    @pl.when(row > 0)
    def _():
        pltpu.make_async_copy(u_recv, u_recv, urecv_sem).wait()

    u = u_recv[...]
    for layer in range(layers):
        load = loads[:, layer * 128 : (layer + 1) * 128]
        rhs = load - (coup[layer, 0:1, :] * u + coup[layer, 1:2, :] * turned(u))
        rhs_v[layer] = rhs.astype(jnp.bfloat16)
        for offset in order:
            pltpu.make_async_remote_copy(
                src_ref=rhs_v.at[layer], dst_ref=gath_v.at[layer, me],
                send_sem=rhs_send.at[layer], recv_sem=rhs_recv.at[layer],
                device_id=(row, peer(offset)), device_id_type=MESH,
            ).start()
        gath_v[layer, me] = rhs_v[layer]
        schur_copies[layer].wait()
        pltpu.make_async_copy(
            gath_v.at[layer, others], gath_v.at[layer, others], rhs_recv.at[layer]
        ).wait()

        def add_chip(chip, total):
            left = jnp.concatenate([gath_v[layer, 2 * chip], gath_v[layer, 2 * chip + 1]], 1)
            rows = pl.ds(pl.multiple_of(chip * 256, 256), 256)
            right = jnp.concatenate([schur_v[layer, 0, rows, :], schur_v[layer, 1, rows, :]], 1)
            return total + jnp.dot(left, right, preferred_element_type=jnp.float32)

        total = lax.fori_loop(0, senders // 2, add_chip, jnp.zeros((8, 256), jnp.float32), unroll=8)
        u = total[:, :128] + turned(total[:, 128:])
        out[layer] = u

    @pl.when(row < 3)
    def _():
        u_send[...] = u
        copy = pltpu.make_async_remote_copy(
            src_ref=u_send, dst_ref=u_recv, send_sem=usend_sem, recv_sem=urecv_sem,
            device_id=(row + 1, me), device_id_type=MESH,
        )
        copy.start()
        copy.wait_send()

    pltpu.make_async_copy(send_v.at[others], send_v.at[others], a2a_send).wait()
    for layer in range(layers):
        pltpu.make_async_copy(
            gath_v.at[layer, others], gath_v.at[layer, others], rhs_send.at[layer]
        ).wait()


def shards(cond_block, interior_src, face_index, owner_count, coupling, schur_inv):
    cond, inter = cond_block[0, 0], interior_src[0, 0]
    face, count = face_index[0, 0], owner_count[0]
    layers, _, trace, width = schur_inv.shape
    peers = face.shape[0]
    vmem = pl.BlockSpec(memory_space=pltpu.VMEM)
    hbm = pl.BlockSpec(memory_space=pl.ANY)
    f32, bf16 = jnp.float32, jnp.bfloat16
    dma = pltpu.SemaphoreType.DMA
    return pl.pallas_call(
        kernel,
        out_shape=jax.ShapeDtypeStruct((layers, 8, width), f32),
        in_specs=[pl.BlockSpec(memory_space=pltpu.SMEM), vmem, vmem, vmem, hbm, hbm],
        out_specs=vmem,
        scratch_shapes=[
            pltpu.VMEM(cond.shape, bf16),
            pltpu.VMEM(schur_inv.shape, bf16),
            pltpu.VMEM((*inter.shape[:3], 128), f32),
            pltpu.VMEM((cond.shape[1], 8, 128), f32),
            pltpu.VMEM((peers, 8, 256), bf16),
            pltpu.VMEM((peers, 8, 256), bf16),
            pltpu.VMEM((peers, layers * width, 256), bf16),
            pltpu.VMEM((layers, 8, width), bf16),
            pltpu.VMEM((layers, peers, 8, width), bf16),
            pltpu.VMEM((8, width), f32),
            pltpu.VMEM((8, width), f32),
            dma((4,)), dma((layers,)), dma, dma, dma((layers,)), dma((layers,)), dma, dma,
        ],
        compiler_params=pltpu.CompilerParams(
            collective_id=0, has_side_effects=True, vmem_limit_bytes=60 << 20
        ),
    )(count, inter, face, coupling, cond, schur_inv)


def solution(mesh):
    placed = (
        P("sweep", "xsec", None, None, None, None),
        P("sweep", "xsec", None, None, None, None),
        P("sweep", "xsec", None, None),
        P("sweep", "xsec", None),
        P("sweep", None, "xsec"),
        P("sweep", None, None, "xsec"),
    )
    return jax.shard_map(
        shards, mesh=mesh, in_specs=placed, out_specs=P("sweep", None, "xsec"), check_vma=False
    )
```

time: 244 us -> 89.4 us (0.37)
  blocking collectives: 110 us -> 0 us
  Pallas kernels: 0 us -> 88 us
  matrix products: 47.7 us -> 0 us
  waiting for transfers between devices: 35.3 us -> 0 us
  local copies, waits for them, and re-layouts: 25.7 us -> 1.3 us
  starting transfers between devices: 22.2 us -> 0 us
    all_to_all x7 -> x0, blocking collectives: 110 us -> none  [copy_for_each(): return lax.all_to_all(copies, axis, split_axis=0, concat_axis=0, tiled=True)]
    pallas_call x0 -> x1, Pallas kernels: none -> 88 us  [shards(): pl.pallas_call(kernel, out_shape=jax.ShapeDtypeStruct((layers, 8, width),...]
    dot_general x28 -> x0, matrix products: 47.7 us -> none  [the longest x8 14.6 us: add_group(): jnp.einsum('cmf,cfz->mz', values_block, onehot, precision=lax.Precision.H...]
    all_to_all x2 -> x0, waiting for transfers between devices: 26.2 us -> none  [the longest x1 15.8 us: shards(): lax.all_to_all(outgoing_rows, 'xsec', split_axis=0, concat_axis=0, tiled=...]
    all_to_all x2 -> x0, starting transfers between devices: 17 us -> none  [the longest x1 12.2 us: shards(): lax.all_to_all(outgoing_rows, 'xsec', split_axis=0, concat_axis=0, tiled=...]
    slice x7 -> x0, local copies, waits for them, and re-layouts: 14.4 us -> none  [the longest x2 7.53 us: shards(): couple_blocks[1]]
    ppermute x4 -> x0, waiting for transfers between devices: 9.16 us -> none  [from_behind(): lax.ppermute(value, axis, [(source, source + steps) for source in range(i...]
    dynamic_slice x16 -> x0, local copies, waits for them, and re-layouts: 5.63 us -> none  [the longest x8 5.62 us: add_group(): index_block = lax.dynamic_slice_in_dim(index_rows, group_at * 8, 8, 0)]
  transfers between devices with their start and end apart: 6 -> 0, of which waited for: 5 -> 0; matrix products, arithmetic and copies ran while one was open for 8% -> 0% of each run, Pallas kernels for 0% -> 0%
where the time goes in v1:
time: 89.4 us; the launch traced here: 89.3 us
  Pallas kernels  88 us (98%)
  local copies, waits for them, and re-layouts  1.3 us (1%)
    pallas_call x1, Pallas kernels, shards(): pl.pallas_call(kernel, out_shape=jax.ShapeDtypeStruct((layers, 8, width),...  88 us

profile of v1, /device:TPU:25, one launch (start us, length us, event | category | flops | bytes accessed | tf_op | source)
XLA Modules:
  0.0 89.3 jit_solution(8594705759650473789)
XLA Ops:
  0.0 88.0 %shard_map.64 = f32[2,8,128]{2,1,0:T(8,128)} custom-call(s32[1,64]{1,0:T(1,128)} %bitcast.7, bf16[2,4,40,512]{3,2,1,0:T(8,128)(2,1)} %bitcast.5, s32[64,192]{1,0:T(8,128)} %bitcast.6, f32[2,2,128]{2,1,0:T(2,128)} %coup.1, bf16[2,24,40,512]{3,2,1,0:T(8,128)(2,1)} %bitcast.4, bf16[2,2,8192,128]{3,2,1,0:T(8,128)(2,1)} %schur.1), custom_call_target="tpu_custom_call" | custom-call | tf_op jit(solution)/shard_map/pallas_call | solution.py:238
  88.0 1.3 %copy.8 = f32[2,8,128]{2,1,0:T(8,128)} copy(f32[2,8,128]{2,1,0:T(8,128)} %shard_map.64) | data formatting | bytes 16384

commit v2 on v1

v2 whole, which is shorter than its diff:
```python
import functools

import jax
import jax.numpy as jnp
from jax import lax
from jax.experimental import pallas as pl
from jax.experimental.pallas import tpu as pltpu
from jax.sharding import PartitionSpec as P

CAP = 8
MESH = pl.DeviceIdType.MESH
NX, NZ = 4, 8
DX_ORDER = (2, 1, 3, 0)
DZ_ORDER = (4, 3, 5, 2, 6, 1, 7, 0)
BARRIER_AT = 1
NEAR = ((0, 2), (3, 3), (4, 4))
VMEM_BYTES = 60 << 20


def hops(offset):
    return min(offset[0], NX - offset[0]) + min(offset[1], NZ - offset[1])


def chips_by_group():
    chips = sorted(((dx, dz) for dx in range(NX) for dz in range(NZ)), key=hops)
    near = [[o for o in chips if low <= hops(o) <= high] for low, high in NEAR]
    return near, [o for o in chips if hops(o) > NEAR[-1][1]]


def opposite(chip):
    return (-chip[0]) % NX, (-chip[1]) % NZ


def peers_far_first():
    offsets = [(dx, dz, dc) for dx in range(NX) for dz in range(NZ) for dc in range(2)]
    offsets.remove((0, 0, 0))
    return sorted(offsets, key=lambda o: -hops(o))


def row_iota(shape):
    return lax.broadcasted_iota(jnp.int32, shape, 0)


def lane_iota(shape):
    return lax.broadcasted_iota(jnp.int32, shape, 1)


def sum_rows(parts):
    rows = row_iota((8, 128))
    top = rows < 4
    level = [
        jnp.where(top, parts[m], parts[m + 4])
        + pltpu.roll(jnp.where(top, parts[m + 4], parts[m]), 4, 0)
        for m in range(4)
    ]
    for step in (2, 1):
        low = (rows & step) == 0
        level = [
            jnp.where(
                low,
                level[m] + pltpu.roll(level[m], 8 - step, 0),
                level[m + step] + pltpu.roll(level[m + step], step, 0),
            )
            for m in range(step)
        ]
    return level[0]


def swap_groups(values, steps):
    groups = lane_iota((8, 128)) // CAP
    values = list(values)
    for step in steps:
        upper = (groups & step) != 0
        for at in range(len(values)):
            if at & step:
                continue
            first, second = values[at], values[at + step]
            values[at] = jnp.where(upper, pltpu.roll(second, step * CAP, 1), first)
            values[at + step] = jnp.where(upper, second, pltpu.roll(first, 128 - step * CAP, 1))
    return values


def kernel(
    count_h, inter_h, face_h, coup_h, cond, schur, out,
    cond_v, schur_v, inter_v, face_v, count_v, coup_v, inter_f, terms, send_v, recv_v, onehot,
    rhs_v, near_v, pass_v, far_v, ahead_send, ahead_recv,
    in_sem, cond_sem, schur_sem, a2a_send, a2a_recv,
    rhs_send, near_recv, pass_send, pass_recv, far_recv, ahead_send_sem, ahead_recv_sem,
):
    me = lax.axis_index("xsec")
    row = lax.axis_index("sweep")
    mx, mz, mc = me // 16, (me // 2) % 8, me % 2
    n_faces = cond.shape[1]
    layers = schur.shape[0]
    senders = recv_v.shape[0]
    slots = onehot.shape[2]

    def tile_of(dx):
        return (mx + dx) % NX

    def peer(offset):
        dx, dz, dc = offset
        return tile_of(dx) * 16 + ((mz + dz) % NZ) * 2 + (mc + dc) % 2

    def lanes_of(dx):
        return pl.ds(pl.multiple_of(tile_of(dx) * 128, 128), 128)

    small_copies = [
        pltpu.make_async_copy(source, target, in_sem.at[at])
        for at, (source, target) in enumerate(
            ((inter_h, inter_v), (face_h, face_v), (count_h, count_v), (coup_h, coup_v))
        )
    ]
    cond_copies = [
        pltpu.make_async_copy(
            cond.at[:, :, :, lanes_of(dx)], cond_v.at[:, :, :, lanes_of(dx)], cond_sem.at[at]
        )
        for at, dx in enumerate(DX_ORDER)
    ]
    schur_copies = [
        pltpu.make_async_copy(schur.at[layer], schur_v.at[layer], schur_sem.at[layer])
        for layer in range(layers)
    ]
    small_copies[0].start()
    for copy in cond_copies + small_copies[1:] + schur_copies:
        copy.start()

    order = peers_far_first()
    barrier = pltpu.get_barrier_semaphore()
    for offset in order:
        pl.semaphore_signal(barrier, inc=1, device_id=(row, peer(offset)), device_id_type=MESH)
    pl.semaphore_signal(barrier, inc=1, device_id=((row + 1) % 4, me), device_id_type=MESH)
    pl.semaphore_signal(barrier, inc=1, device_id=((row + 3) % 4, me), device_id_type=MESH)

    def send_tile(at):
        dx = DX_ORDER[at]
        for dz in DZ_ORDER:
            for dc in range(2):
                if (dx, dz, dc) == (0, 0, 0):
                    continue
                target = peer((dx, dz, dc))
                pltpu.make_async_remote_copy(
                    src_ref=send_v.at[target], dst_ref=recv_v.at[me],
                    send_sem=a2a_send, recv_sem=a2a_recv.at[at],
                    device_id=(row, target), device_id_type=MESH,
                ).start()

    small_copies[0].wait()
    for at, dx in enumerate(DX_ORDER):
        lanes = lanes_of(dx)
        inter_f[...] = inter_v[:, :, :, lanes].astype(jnp.float32)
        cond_copies[at].wait()

        def one_face(k, carry):
            real = cond_v[0, k, :, lanes].astype(jnp.float32)
            imag = cond_v[1, k, :, lanes].astype(jnp.float32)

            def fold(value):
                return sum(value[8 * v : 8 * v + 8] for v in range(value.shape[0] // 8))

            real_parts = [fold(real * inter_f[0, j] - imag * inter_f[1, j]) for j in range(4)]
            imag_parts = [fold(real * inter_f[1, j] + imag * inter_f[0, j]) for j in range(4)]
            terms[k] = sum_rows(real_parts + imag_parts)
            return carry

        lax.fori_loop(0, n_faces, one_face, 0, unroll=4)
        first = swap_groups([terms[k] for k in range(16)], (8, 4, 2, 1))
        second = swap_groups([terms[k] for k in range(16, 24)], (4, 2, 1))
        base = tile_of(dx) * 16
        left = lane_iota((8, 128)) < 64
        for d in range(16):
            value = second[d % 8]
            if d < 8:
                tail = jnp.where(left, value, pltpu.roll(pltpu.roll(value, 64, 1), 4, 0))
            else:
                tail = jnp.where(left, pltpu.roll(value, 64, 1), pltpu.roll(value, 4, 0))
            send_v[base + d, 0] = first[d][:4].astype(jnp.bfloat16)
            send_v[base + d, 1] = first[d][4:].astype(jnp.bfloat16)
            send_v[base + d, 2] = tail[:4].astype(jnp.bfloat16)
        if at == BARRIER_AT:
            pl.semaphore_wait(barrier, len(order) + 2)
            for earlier in range(at):
                send_tile(earlier)
        if at >= BARRIER_AT:
            send_tile(at)
    recv_v[me] = send_v[me]

    for copy in small_copies[1:]:
        copy.wait()
    n_rows = n_faces * CAP
    index = jnp.concatenate(
        [face_v[...], jnp.zeros((senders, 256 - n_rows), jnp.int32)], 1
    )
    index = jnp.concatenate([index, jnp.zeros((128 - senders, 256), jnp.int32)], 0)
    index = jnp.concatenate([index[:, :128].T, index[:, 128:].T], 0)[:n_rows]
    counts = jnp.concatenate([count_v[...], jnp.zeros((1, 128 - senders), jnp.int32)], 1)
    index = jnp.where(row_iota((n_rows, 128)) % CAP < counts, index, -1)
    index = index.astype(jnp.float32).astype(jnp.bfloat16)
    unknown = lane_iota((n_rows, slots)).astype(jnp.float32).astype(jnp.bfloat16)
    one, zero = jnp.ones((), jnp.bfloat16), jnp.zeros((), jnp.bfloat16)

    for c in range(senders):
        onehot[c] = jnp.where(index[:, c : c + 1] == unknown, one, zero)

    def add_sender(c, total):
        top, bottom, tail = (recv_v[c, part].astype(jnp.float32) for part in range(3))
        head = jnp.concatenate([top, bottom], 0)
        tail = jnp.concatenate([tail[:, :64], tail[:, 64:]], 0)
        block = jnp.concatenate([head, tail], 1).astype(jnp.bfloat16)
        return total + jnp.dot(block, onehot[c], preferred_element_type=jnp.float32)

    loads = jnp.zeros((8, slots), jnp.float32)
    for at, dx in enumerate(DX_ORDER):
        some = recv_v.at[pl.ds(0, 16 if dx else 15)]
        pltpu.make_async_copy(some, some, a2a_recv.at[at]).wait()
        start = tile_of(NX - dx) * 16
        loads = lax.fori_loop(
            0, 16, lambda i, total: add_sender(start + i, total), loads, unroll=8
        )

    sign = jnp.where(row_iota((8, 128)) < 4, -1.0, 1.0)
    groups, far = chips_by_group()
    starts = [sum(len(g) for g in groups[:at]) for at in range(len(groups))]
    near = [chip for group in groups for chip in group]

    def turned(value):
        return sign * pltpu.roll(value, 4, 0)

    def right_side(load, couple, u):
        return load - (couple[0:1] * u + couple[1:2] * turned(u))

    def send_rhs(at, layer, to_row, own):
        source = rhs_v.at[at]

        def start(target, dst, sem):
            pltpu.make_async_remote_copy(
                src_ref=source, dst_ref=dst, send_sem=rhs_send.at[at], recv_sem=sem,
                device_id=(to_row, target), device_id_type=MESH,
            ).start()

        for chip in reversed(far):
            slot = 2 * far.index(opposite(chip)) + mc
            for dc in range(2):
                start(peer((*chip, dc)), far_v.at[layer, slot], far_recv.at[layer])
        for chip in reversed(near):
            slot = near.index(opposite(chip))
            group = max(g for g in range(len(groups)) if starts[g] <= slot)
            if chip != (0, 0) or not own:
                start(peer((*chip, 0)), near_v.at[layer, slot], near_recv.at[layer, group])
        if own:
            pltpu.make_async_copy(source, near_v.at[layer, 0], near_recv.at[layer, 0]).start()

    remote_near, remote_far = len(near) - 1, 2 * len(far)

    def solve(layer):
        partner = peer((0, 0, 1))
        passes = []
        schur_copies[layer].wait()
        total = jnp.zeros((8, 256), jnp.float32)

        def rows_of(chip, core):
            first = (tile_of(chip[0]) * 8 + (mz + chip[1]) % NZ) * 256 + core * 128
            rows = pl.ds(pl.multiple_of(first, 128), 128)
            return jnp.concatenate([schur_v[layer, 0, rows, :], schur_v[layer, 1, rows, :]], 1)

        def add_blocks(total, blocks):
            while len(blocks) >= 2:
                pair, blocks = blocks[:2], blocks[2:]
                left = jnp.concatenate([ref[layer, slot] for ref, slot, _, _ in pair], 1)
                right = jnp.concatenate([rows_of(chip, core) for _, _, chip, core in pair], 0)
                total = total + jnp.dot(left, right, preferred_element_type=jnp.float32)
            return total, blocks

        left_over = []
        for at, group in enumerate(groups):
            part = pl.ds(starts[at], len(group))
            some = near_v.at[layer, part]
            pltpu.make_async_copy(some, some, near_recv.at[layer, at]).wait()
            passes.append(
                pltpu.make_async_remote_copy(
                    src_ref=some, dst_ref=pass_v.at[layer, part],
                    send_sem=pass_send.at[layer, at], recv_sem=pass_recv.at[layer, at],
                    device_id=(row, partner), device_id_type=MESH,
                )
            )
            passes[-1].start()
            blocks = [(near_v, near.index(chip), chip, mc) for chip in group]
            total, left_over = add_blocks(total, left_over + blocks)
        def add_passed(total, left_over, at):
            passes[at].wait_recv()
            blocks = [(pass_v, near.index(chip), chip, 1 - mc) for chip in groups[at]]
            return add_blocks(total, left_over + blocks)

        for at in range(len(groups) - 1):
            total, left_over = add_passed(total, left_over, at)
        some = far_v.at[layer]
        pltpu.make_async_copy(some, some, far_recv.at[layer]).wait()
        blocks = [(far_v, 2 * at + core, chip, core) for at, chip in enumerate(far) for core in (0, 1)]
        total, left_over = add_blocks(total, left_over + blocks)
        total, left_over = add_passed(total, left_over, len(groups) - 1)
        assert not left_over
        u = total[:, :128] + turned(total[:, 128:])
        out[layer] = u
        return u, passes

    ahead_send[0:8, :] = loads[:, :128]
    ahead_send[8:10, :] = coup_v[0]
    ahead = pltpu.make_async_remote_copy(
        src_ref=ahead_send, dst_ref=ahead_recv, send_sem=ahead_send_sem,
        recv_sem=ahead_recv_sem, device_id=(row - 1, me), device_id_type=MESH,
    )

    @pl.when(row > 0)
    def _():
        ahead.start()

    @pl.when(row == 0)
    def _():
        zero = jnp.zeros((8, 128), jnp.float32)
        rhs_v[0] = right_side(loads[:, :128], coup_v[0], zero).astype(jnp.bfloat16)
        send_rhs(0, 0, row, True)

    u, passes_0 = solve(0)
    rhs_v[1] = right_side(loads[:, 128:], coup_v[1], u).astype(jnp.bfloat16)
    send_rhs(1, 1, row, True)
    u, passes_1 = solve(1)

    @pl.when(row < 3)
    def _():
        pltpu.make_async_copy(ahead_recv, ahead_recv, ahead_recv_sem).wait()
        rhs = right_side(ahead_recv[0:8, :], ahead_recv[8:10, :], u)
        rhs_v[2] = rhs.astype(jnp.bfloat16)
        send_rhs(2, 0, row + 1, False)

    others = pl.ds(0, senders - 1)
    pltpu.make_async_copy(send_v.at[others], send_v.at[others], a2a_send).wait()
    for copy in passes_0 + passes_1:
        copy.wait_send()

    def wait_sent(at, count):
        some = near_v.reshape(-1, 8, 128).at[pl.ds(0, count)]
        pltpu.make_async_copy(some, some, rhs_send.at[at]).wait()

    wait_sent(1, remote_near + remote_far)

    @pl.when(row > 0)
    def _():
        ahead.wait_send()

    @pl.when(row == 0)
    def _():
        wait_sent(0, remote_near + remote_far)

    @pl.when(row < 3)
    def _():
        wait_sent(2, remote_near + 1 + remote_far)


def shards(cond_block, interior_src, face_index, owner_count, coupling, schur_inv):
    cond, inter = cond_block[0, 0], interior_src[0, 0]
    face, count = face_index[0, 0], owner_count[0]
    layers, _, trace, width = schur_inv.shape
    peers = face.shape[0]
    near, far = (sum(map(len, chips_by_group()[0])), len(chips_by_group()[1]))
    vmem = pl.BlockSpec(memory_space=pltpu.VMEM)
    hbm = pl.BlockSpec(memory_space=pl.ANY)
    f32, bf16 = jnp.float32, jnp.bfloat16
    dma = pltpu.SemaphoreType.DMA
    return pl.pallas_call(
        kernel,
        out_shape=jax.ShapeDtypeStruct((layers, 8, width), f32),
        in_specs=[hbm] * 6,
        out_specs=vmem,
        scratch_shapes=[
            pltpu.VMEM(cond.shape, bf16),
            pltpu.VMEM(schur_inv.shape, bf16),
            pltpu.VMEM(inter.shape, bf16),
            pltpu.VMEM(face.shape, jnp.int32),
            pltpu.VMEM(count.shape, jnp.int32),
            pltpu.VMEM(coupling.shape, f32),
            pltpu.VMEM((*inter.shape[:3], 128), f32),
            pltpu.VMEM((cond.shape[1], 8, 128), f32),
            pltpu.VMEM((peers, 3, 4, 128), bf16),
            pltpu.VMEM((peers, 3, 4, 128), bf16),
            pltpu.VMEM((peers, face.shape[1], layers * width), bf16),
            pltpu.VMEM((layers + 1, 8, width), bf16),
            pltpu.VMEM((layers, near, 8, width), bf16),
            pltpu.VMEM((layers, near, 8, width), bf16),
            pltpu.VMEM((layers, 2 * far, 8, width), bf16),
            pltpu.VMEM((10, width), f32),
            pltpu.VMEM((10, width), f32),
            dma((4,)), dma((4,)), dma((layers,)), dma, dma((4,)),
            dma((layers + 1,)), dma((layers, len(NEAR))), dma((layers, len(NEAR))),
            dma((layers, len(NEAR))), dma((layers,)), dma, dma,
        ],
        compiler_params=pltpu.CompilerParams(
            collective_id=0, has_side_effects=True, vmem_limit_bytes=VMEM_BYTES
        ),
    )(count, inter, face, coupling, cond, schur_inv)


def solution(mesh):
    placed = (
        P("sweep", "xsec", None, None, None, None),
        P("sweep", "xsec", None, None, None, None),
        P("sweep", "xsec", None, None),
        P("sweep", "xsec", None),
        P("sweep", None, "xsec"),
        P("sweep", None, None, "xsec"),
    )
    return jax.shard_map(
        shards, mesh=mesh, in_specs=placed, out_specs=P("sweep", None, "xsec"), check_vma=False
    )
```

time: 89.4 us -> 77.7 us (0.87)
  Pallas kernels: 88 us -> 76.3 us
    pallas_call x1, Pallas kernels: 88 us -> 76.3 us  [shards(): pl.pallas_call(kernel, out_shape=jax.ShapeDtypeStruct((layers, 8, width),...]
where the time goes in v2:
time: 77.7 us; the launch traced here: 77.6 us
  Pallas kernels  76.3 us (98%)
  local copies, waits for them, and re-layouts  1.3 us (2%)
    pallas_call x1, Pallas kernels, shards(): pl.pallas_call(kernel, out_shape=jax.ShapeDtypeStruct((layers, 8, width),...  76.3 us

profile of v2, /device:TPU:25, one launch (start us, length us, event | category | flops | bytes accessed | tf_op | source)
XLA Modules:
  0.0 77.6 jit_solution(1656908255777725065)
XLA Ops:
  0.0 76.3 %shard_map.64 = f32[2,8,128]{2,1,0:T(8,128)} custom-call(s32[1,64]{1,0:T(1,128)} %bitcast.7, bf16[2,4,40,512]{3,2,1,0:T(8,128)(2,1)} %bitcast.5, s32[64,192]{1,0:T(8,128)} %bitcast.6, f32[2,2,128]{2,1,0:T(2,128)} %coup_h.1, bf16[2,24,40,512]{3,2,1,0:T(8,128)(2,1)} %bitcast.4, bf16[2,2,8192,128]{3,2,1,0:T(8,128)(2,1)} %schur.1), custom_call_target="tpu_custom_call" | custom-call | tf_op jit(solution)/shard_map/pallas_call | solution.py:369
  76.3 1.3 %copy.8 = f32[2,8,128]{2,1,0:T(8,128)} copy(f32[2,8,128]{2,1,0:T(8,128)} %shard_map.64) | data formatting | bytes 16384

commit v3 on v2

--- a/solution.py
+++ b/solution.py
@@ -83,7 +83,7 @@
 def kernel(
     count_h, inter_h, face_h, coup_h, cond, schur, out,
     cond_v, schur_v, inter_v, face_v, count_v, coup_v, inter_f, terms, send_v, recv_v, onehot,
-    rhs_v, near_v, pass_v, far_v, ahead_send, ahead_recv,
+    rhs_v, near_v, pass_v, far_v, stage_v, u_v,
     in_sem, cond_sem, schur_sem, a2a_send, a2a_recv,
     rhs_send, near_recv, pass_send, pass_recv, far_recv, ahead_send_sem, ahead_recv_sem,
 ):
@@ -117,12 +117,12 @@
         )
         for at, dx in enumerate(DX_ORDER)
     ]
-    schur_copies = [
-        pltpu.make_async_copy(schur.at[layer], schur_v.at[layer], schur_sem.at[layer])
-        for layer in range(layers)
-    ]
+
+    def schur_copy(layer):
+        return pltpu.make_async_copy(schur.at[layer], schur_v.at[layer], schur_sem.at[layer])
+
     small_copies[0].start()
-    for copy in cond_copies + small_copies[1:] + schur_copies:
+    for copy in cond_copies + small_copies[1:] + [schur_copy(layer) for layer in range(layers)]:
         copy.start()
 
     order = peers_far_first()
@@ -195,12 +195,17 @@
     index = jnp.concatenate([index[:, :128].T, index[:, 128:].T], 0)[:n_rows]
     counts = jnp.concatenate([count_v[...], jnp.zeros((1, 128 - senders), jnp.int32)], 1)
     index = jnp.where(row_iota((n_rows, 128)) % CAP < counts, index, -1)
-    index = index.astype(jnp.float32).astype(jnp.bfloat16)
+    index = index.astype(jnp.float32)
     unknown = lane_iota((n_rows, slots)).astype(jnp.float32).astype(jnp.bfloat16)
     one, zero = jnp.ones((), jnp.bfloat16), jnp.zeros((), jnp.bfloat16)
 
-    for c in range(senders):
-        onehot[c] = jnp.where(index[:, c : c + 1] == unknown, one, zero)
+    def some_senders(at, index):
+        for c in range(8):
+            column = index[:, c : c + 1].astype(jnp.bfloat16)
+            onehot[8 * at + c] = jnp.where(column == unknown, one, zero)
+        return pltpu.roll(index, 120, 1)
+
+    lax.fori_loop(0, senders // 8, some_senders, index)
 
     def add_sender(c, total):
         top, bottom, tail = (recv_v[c, part].astype(jnp.float32) for part in range(3))
@@ -229,33 +234,47 @@
     def right_side(load, couple, u):
         return load - (couple[0:1] * u + couple[1:2] * turned(u))
 
-    def send_rhs(at, layer, to_row, own):
-        source = rhs_v.at[at]
+    def send_rhs(stage, layer, to_row, own):
+        source = rhs_v.at[stage]
 
         def start(target, dst, sem):
             pltpu.make_async_remote_copy(
-                src_ref=source, dst_ref=dst, send_sem=rhs_send.at[at], recv_sem=sem,
+                src_ref=source, dst_ref=dst, send_sem=rhs_send.at[stage], recv_sem=sem,
                 device_id=(to_row, target), device_id_type=MESH,
             ).start()
 
+        def send_near(chips):
+            for chip in chips:
+                slot = near.index(opposite(chip))
+                group = max(g for g in range(len(groups)) if starts[g] <= slot)
+                start(peer((*chip, 0)), near_v.at[layer, slot], near_recv.at[layer, group])
+
+        send_near(groups[-1])
         for chip in reversed(far):
             slot = 2 * far.index(opposite(chip)) + mc
             for dc in range(2):
                 start(peer((*chip, dc)), far_v.at[layer, slot], far_recv.at[layer])
-        for chip in reversed(near):
-            slot = near.index(opposite(chip))
-            group = max(g for g in range(len(groups)) if starts[g] <= slot)
-            if chip != (0, 0) or not own:
-                start(peer((*chip, 0)), near_v.at[layer, slot], near_recv.at[layer, group])
-        if own:
+        send_near(near[len(near) - len(groups[-1]) - 1 : 0 : -1])
+
+        @pl.when(own)
+        def _():
             pltpu.make_async_copy(source, near_v.at[layer, 0], near_recv.at[layer, 0]).start()
 
-    remote_near, remote_far = len(near) - 1, 2 * len(far)
+        @pl.when(jnp.logical_not(own))
+        def _():
+            start(me, near_v.at[layer, 0], near_recv.at[layer, 0])
+
+    def passing(layer, group):
+        part = pl.ds(starts[group], len(groups[group]))
+        return pltpu.make_async_remote_copy(
+            src_ref=near_v.at[layer, part], dst_ref=pass_v.at[layer, part],
+            send_sem=pass_send.at[layer, group], recv_sem=pass_recv.at[layer, group],
+            device_id=(row, peer((0, 0, 1))), device_id_type=MESH,
+        )
 
     def solve(layer):
-        partner = peer((0, 0, 1))
         passes = []
-        schur_copies[layer].wait()
+        schur_copy(layer).wait()
         total = jnp.zeros((8, 256), jnp.float32)
 
         def rows_of(chip, core):
@@ -276,13 +295,7 @@
             part = pl.ds(starts[at], len(group))
             some = near_v.at[layer, part]
             pltpu.make_async_copy(some, some, near_recv.at[layer, at]).wait()
-            passes.append(
-                pltpu.make_async_remote_copy(
-                    src_ref=some, dst_ref=pass_v.at[layer, part],
-                    send_sem=pass_send.at[layer, at], recv_sem=pass_recv.at[layer, at],
-                    device_id=(row, partner), device_id_type=MESH,
-                )
-            )
+            passes.append(passing(layer, at))
             passes[-1].start()
             blocks = [(near_v, near.index(chip), chip, mc) for chip in group]
             total, left_over = add_blocks(total, left_over + blocks)
@@ -301,12 +314,13 @@
         assert not left_over
         u = total[:, :128] + turned(total[:, 128:])
         out[layer] = u
-        return u, passes
-
-    ahead_send[0:8, :] = loads[:, :128]
-    ahead_send[8:10, :] = coup_v[0]
+        u_v[...] = u
+
+    for layer in range(layers):
+        stage_v[layer, 0:8, :] = loads[:, layer * 128 : (layer + 1) * 128]
+        stage_v[layer, 8:10, :] = coup_v[layer]
     ahead = pltpu.make_async_remote_copy(
-        src_ref=ahead_send, dst_ref=ahead_recv, send_sem=ahead_send_sem,
+        src_ref=stage_v.at[0], dst_ref=stage_v.at[layers], send_sem=ahead_send_sem,
         recv_sem=ahead_recv_sem, device_id=(row - 1, me), device_id_type=MESH,
     )
 
@@ -314,34 +328,41 @@
     def _():
         ahead.start()
 
-    @pl.when(row == 0)
-    def _():
-        zero = jnp.zeros((8, 128), jnp.float32)
-        rhs_v[0] = right_side(loads[:, :128], coup_v[0], zero).astype(jnp.bfloat16)
-        send_rhs(0, 0, row, True)
-
-    u, passes_0 = solve(0)
-    rhs_v[1] = right_side(loads[:, 128:], coup_v[1], u).astype(jnp.bfloat16)
-    send_rhs(1, 1, row, True)
-    u, passes_1 = solve(1)
-
-    @pl.when(row < 3)
-    def _():
-        pltpu.make_async_copy(ahead_recv, ahead_recv, ahead_recv_sem).wait()
-        rhs = right_side(ahead_recv[0:8, :], ahead_recv[8:10, :], u)
-        rhs_v[2] = rhs.astype(jnp.bfloat16)
-        send_rhs(2, 0, row + 1, False)
+    u_v[...] = jnp.zeros_like(u_v)
+
+    def one_stage(stage, carry):
+        @pl.when(stage > 0)
+        def _():
+            solve(stage - 1)
+
+        last = stage == layers
+
+        @pl.when(((stage > 0) | (row == 0)) & (jnp.logical_not(last) | (row < 3)))
+        def _():
+            @pl.when(last)
+            def _():
+                pltpu.make_async_copy(stage_v.at[0], stage_v.at[layers], ahead_recv_sem).wait()
+
+            rhs = right_side(stage_v[stage, 0:8, :], stage_v[stage, 8:10, :], u_v[...])
+            rhs_v[stage] = rhs.astype(jnp.bfloat16)
+            send_rhs(stage, stage % layers, row + stage // layers, jnp.logical_not(last))
+
+        return carry
+
+    lax.fori_loop(0, layers + 1, one_stage, 0)
 
     others = pl.ds(0, senders - 1)
     pltpu.make_async_copy(send_v.at[others], send_v.at[others], a2a_send).wait()
-    for copy in passes_0 + passes_1:
-        copy.wait_send()
-
-    def wait_sent(at, count):
+    for layer in range(layers):
+        for group in range(len(groups)):
+            passing(layer, group).wait_send()
+
+    def wait_sent(stage, count):
         some = near_v.reshape(-1, 8, 128).at[pl.ds(0, count)]
-        pltpu.make_async_copy(some, some, rhs_send.at[at]).wait()
-
-    wait_sent(1, remote_near + remote_far)
+        pltpu.make_async_copy(some, some, rhs_send.at[stage]).wait()
+
+    remote = len(near) - 1 + 2 * len(far)
+    wait_sent(1, remote)
 
     @pl.when(row > 0)
     def _():
@@ -349,11 +370,11 @@
 
     @pl.when(row == 0)
     def _():
-        wait_sent(0, remote_near + remote_far)
+        wait_sent(0, remote)
 
     @pl.when(row < 3)
     def _():
-        wait_sent(2, remote_near + 1 + remote_far)
+        wait_sent(2, remote + 1)
 
 
 def shards(cond_block, interior_src, face_index, owner_count, coupling, schur_inv):
@@ -368,7 +389,7 @@
     dma = pltpu.SemaphoreType.DMA
     return pl.pallas_call(
         kernel,
-        out_shape=jax.ShapeDtypeStruct((layers, 8, width), f32),
+        out_shape=pltpu.VMEM((layers, 8, width), f32),
         in_specs=[hbm] * 6,
         out_specs=vmem,
         scratch_shapes=[
@@ -387,8 +408,8 @@
             pltpu.VMEM((layers, near, 8, width), bf16),
             pltpu.VMEM((layers, near, 8, width), bf16),
             pltpu.VMEM((layers, 2 * far, 8, width), bf16),
-            pltpu.VMEM((10, width), f32),
-            pltpu.VMEM((10, width), f32),
+            pltpu.VMEM((layers + 1, 10, width), f32),
+            pltpu.VMEM((8, width), f32),
             dma((4,)), dma((4,)), dma((layers,)), dma, dma((4,)),
             dma((layers + 1,)), dma((layers, len(NEAR))), dma((layers, len(NEAR))),
             dma((layers, len(NEAR))), dma((layers,)), dma, dma,

time: 77.7 us -> 76.2 us (0.981)
  no operation moved by 1% of the time
where the time goes in v3:
time: 76.2 us
  Pallas kernels  75.6 us (99%)
    pallas_call x1, Pallas kernels, shards(): pl.pallas_call(kernel, out_shape=pltpu.VMEM((layers, 8, width), f32), in_...  75.6 us

profile of v3, /device:TPU:25, one launch (start us, length us, event | category | flops | bytes accessed | tf_op | source)
XLA Modules:
  0.0 76.2 jit_solution(15301962778303006959)
XLA Ops:
  0.0 75.6 %shard_map.64 = f32[2,8,128]{2,1,0:T(8,128)S(1)} custom-call(s32[1,64]{1,0:T(1,128)} %bitcast.7, bf16[2,4,40,512]{3,2,1,0:T(8,128)(2,1)} %bitcast.5, s32[64,192]{1,0:T(8,128)} %bitcast.6, f32[2,2,128]{2,1,0:T(2,128)} %coup_h.1, bf16[2,24,40,512]{3,2,1,0:T(8,128)(2,1)} %bitcast.4, bf16[2,2,8192,128]{3,2,1,0:T(8,128)(2,1)} %schur.1), custom_call_target="tpu_custom_call" | custom-call | tf_op jit(solution)/shard_map/pallas_call | solution.py:390
  75.6 0.6 copy.8

commit v4 on v3

--- a/solution.py
+++ b/solution.py
@@ -13,7 +13,7 @@
 DX_ORDER = (2, 1, 3, 0)
 DZ_ORDER = (4, 3, 5, 2, 6, 1, 7, 0)
 BARRIER_AT = 1
-NEAR = ((0, 2), (3, 3), (4, 4))
+NEAR = ((0, 3), (4, 4))
 VMEM_BYTES = 60 << 20
 
 
@@ -297,8 +297,8 @@
             pltpu.make_async_copy(some, some, near_recv.at[layer, at]).wait()
             passes.append(passing(layer, at))
             passes[-1].start()
-            blocks = [(near_v, near.index(chip), chip, mc) for chip in group]
-            total, left_over = add_blocks(total, left_over + blocks)
+            left_over = left_over + [(near_v, near.index(chip), chip, mc) for chip in group]
+        total, left_over = add_blocks(total, left_over)
         def add_passed(total, left_over, at):
             passes[at].wait_recv()
             blocks = [(pass_v, near.index(chip), chip, 1 - mc) for chip in groups[at]]
@@ -308,9 +308,10 @@
             total, left_over = add_passed(total, left_over, at)
         some = far_v.at[layer]
         pltpu.make_async_copy(some, some, far_recv.at[layer]).wait()
+        passes[-1].wait_recv()
         blocks = [(far_v, 2 * at + core, chip, core) for at, chip in enumerate(far) for core in (0, 1)]
+        blocks += [(pass_v, near.index(chip), chip, 1 - mc) for chip in groups[-1]]
         total, left_over = add_blocks(total, left_over + blocks)
-        total, left_over = add_passed(total, left_over, len(groups) - 1)
         assert not left_over
         u = total[:, :128] + turned(total[:, 128:])
         out[layer] = u

time: 76.2 us -> 75.3 us (0.988)
  Pallas kernels: 75.6 us -> 74.6 us
    pallas_call x1, Pallas kernels: 75.6 us -> 74.6 us  [shards(): pl.pallas_call(kernel, out_shape=pltpu.VMEM((layers, 8, width), f32), in_...]
where the time goes in v4:
time: 75.3 us; the launch traced here: 75.2 us
  Pallas kernels  74.6 us (99%)
    pallas_call x1, Pallas kernels, shards(): pl.pallas_call(kernel, out_shape=pltpu.VMEM((layers, 8, width), f32), in_...  74.6 us

profile of v4, /device:TPU:25, one launch (start us, length us, event | category | flops | bytes accessed | tf_op | source)
XLA Modules:
  0.0 75.2 jit_solution(6996764751558413398)
XLA Ops:
  0.0 74.6 %shard_map.64 = f32[2,8,128]{2,1,0:T(8,128)S(1)} custom-call(s32[1,64]{1,0:T(1,128)} %bitcast.7, bf16[2,4,40,512]{3,2,1,0:T(8,128)(2,1)} %bitcast.5, s32[64,192]{1,0:T(8,128)} %bitcast.6, f32[2,2,128]{2,1,0:T(2,128)} %coup_h.1, bf16[2,24,40,512]{3,2,1,0:T(8,128)(2,1)} %bitcast.4, bf16[2,2,8192,128]{3,2,1,0:T(8,128)(2,1)} %schur.1), custom_call_target="tpu_custom_call" | custom-call | tf_op jit(solution)/shard_map/pallas_call | solution.py:391
  74.6 0.6 copy.8

commit v5 on v4

--- a/solution.py
+++ b/solution.py
@@ -122,8 +122,7 @@
         return pltpu.make_async_copy(schur.at[layer], schur_v.at[layer], schur_sem.at[layer])
 
     small_copies[0].start()
-    for copy in cond_copies + small_copies[1:] + [schur_copy(layer) for layer in range(layers)]:
-        copy.start()
+    cond_copies[0].start()
 
     order = peers_far_first()
     barrier = pltpu.get_barrier_semaphore()
@@ -131,6 +130,9 @@
         pl.semaphore_signal(barrier, inc=1, device_id=(row, peer(offset)), device_id_type=MESH)
     pl.semaphore_signal(barrier, inc=1, device_id=((row + 1) % 4, me), device_id_type=MESH)
     pl.semaphore_signal(barrier, inc=1, device_id=((row + 3) % 4, me), device_id_type=MESH)
+
+    for copy in cond_copies[1:] + small_copies[1:] + [schur_copy(layer) for layer in range(layers)]:
+        copy.start()
 
     def send_tile(at):
         dx = DX_ORDER[at]

time: 75.3 us -> 75 us (level)
  no operation moved by 1% of the time
where the time goes in v5:
time: 75 us
  Pallas kernels  74.4 us (99%)
    pallas_call x1, Pallas kernels, shards(): pl.pallas_call(kernel, out_shape=pltpu.VMEM((layers, 8, width), f32), in_...  74.4 us

profile of v5, /device:TPU:25, one launch (start us, length us, event | category | flops | bytes accessed | tf_op | source)
XLA Modules:
  0.0 75.0 jit_solution(10543245531666427062)
XLA Ops:
  0.0 74.4 %shard_map.64 = f32[2,8,128]{2,1,0:T(8,128)S(1)} custom-call(s32[1,64]{1,0:T(1,128)} %bitcast.7, bf16[2,4,40,512]{3,2,1,0:T(8,128)(2,1)} %bitcast.5, s32[64,192]{1,0:T(8,128)} %bitcast.6, f32[2,2,128]{2,1,0:T(2,128)} %coup_h.1, bf16[2,24,40,512]{3,2,1,0:T(8,128)(2,1)} %bitcast.4, bf16[2,2,8192,128]{3,2,1,0:T(8,128)(2,1)} %schur.1), custom_call_target="tpu_custom_call" | custom-call | tf_op jit(solution)/shard_map/pallas_call | solution.py:393
  74.4 0.6 copy.8
